TPU v7x, 32 devices: a whole 2x2x4 slice. The times are simulated.
32 devices in a mesh: lon: 8 (over z, y), lat: 4 (over x, core).
Axes of the slice: x: 2, y: 2, z: 4, core: 2. Of those that a mesh axis runs over, the one named last changes fastest.
Arguments:
- velocity: bfloat16 [3, 75, 128, 2048], P(None, None, 'lat', 'lon'), may hold values from -1.5 to 1.5
- offsets: float32 [3, 4, 6144], P(None, 'lat', 'lon'), may hold values from 0 to 1
- cells: int32 [3, 4, 6144], P(None, 'lat', 'lon'), may hold values from 0 to 255, as said below
- counts: int32 [4, 8], P('lat', 'lon'), may hold values from 192 to 576, as said below
- moves: int32 [4, 6144], P('lat', 'lon'), may hold values from 0 to 4, as said below
Outputs:
- new_offsets: float32 [3, 4, 6144], P(None, 'lat', 'lon')
- new_cells: int32 [3, 4, 6144], P(None, 'lat', 'lon')
- new_counts: int32 [4, 8], P('lat', 'lon')
Inputs may be any that keep to these rules, and one draw needn't show every extreme that they name: `cells`: values from 0 to 255, 31 and 73 for i, j, k. A valid slot with move 1 has i = 255, move 2 i = 0, move 3 j = 31, move 4 j = 0. `counts`: between 192 and 576; the upper bound is reached by some tile in every draw. `moves`: invalid slots have 0. In each tile at most 48 valid particles have each nonzero move, and in every draw some tile has exactly 48 for each move. Tiles of row 0 have no move 4.
All inputs are finite; a program needn't handle non-finite values.
Results may differ from a plain program's by a relative error of at most 0.00093.
Values may be sent and summed in bfloat16 or wider, within the bound.
No kernel may reach another device: no remote copies, remote signals or barrier semaphores. Data moves between devices by JAX's collectives and lax.ppermute only.
A program may use at most 64 MiB of HBM per device.

v0:
```python
import functools

import jax
import jax.numpy as jnp
from jax import lax
from jax.experimental import pallas as pl
from jax.experimental.pallas import tpu as pltpu
from jax.sharding import PartitionSpec as P

CAP = 48
LANES = 128
HALF = 64
REC = 16
UNROLL = 16
F32, BF16, I32 = jnp.float32, jnp.bfloat16, jnp.int32
VMEM = pl.BlockSpec(memory_space=pltpu.VMEM)
SMEM = pl.BlockSpec(memory_space=pltpu.SMEM)
HBM = pl.BlockSpec(memory_space=pltpu.HBM)


def room(mib):
    return pltpu.CompilerParams(vmem_limit_bytes=mib << 20)


def up8(n):
    return (n + 7) // 8 * 8


def odd_stride(depth):
    lines = 3 * depth + 8
    return lines + 1 - lines % 2


def iota(shape, dim):
    return lax.broadcasted_iota(I32, shape, dim)


def nt(a, b):
    return lax.dot_general(a, b, (((1,), (1,)), ((), ())), preferred_element_type=F32)


def pieces(value):
    high = value.astype(BF16).astype(F32)
    rest = value - high
    middle = rest.astype(BF16).astype(F32)
    return [high, middle, rest - middle]


def decode(x):
    return [x[0:1] + x[1:2] + x[2:3], x[3:4] + x[4:5] + x[5:6], x[6:7] + x[7:8] + x[8:9]]


def pack_kernel(
    vel, off, cel, counts, moves, q1, q2, lonrec, record, rank0, number,
    low, high, offv, celv, movev, strips, recs, sems, small,
):
    depth, rows = vel.shape[1], vel.shape[2]
    tiles = vel.shape[3] // LANES
    slots = off.shape[2]
    stride = odd_stride(depth)
    planes = up8(3 * depth)
    inputs = [
        pltpu.make_async_copy(source, target, small.at[n])
        for n, (source, target) in enumerate(((off, offv), (cel, celv), (moves, movev)))
    ]
    for copy in inputs:
        copy.start()
    copies = []
    for comp in range(3):
        copies.append(
            pltpu.make_async_copy(vel.at[comp, :, pl.ds(0, 8), :], low.at[comp], sems.at[0, comp])
        )
        copies.append(
            pltpu.make_async_copy(
                vel.at[comp, :, pl.ds(rows - 8, 8), :], high.at[comp], sems.at[1, comp]
            )
        )
    for copy in copies:
        copy.start()
    for copy in inputs:
        copy.wait()
    live = counts[0, 0]
    rows_of = []
    for d in range(3):
        rows_of += pieces(offv[d])
    for d in range(3):
        rows_of.append(celv[d].astype(F32))
    rows_of.append(jnp.ones((1, slots), F32))
    for n, row in enumerate(rows_of):
        recs[n : n + 1, :] = row
    recs[len(rows_of) :, :] = jnp.zeros((REC - len(rows_of), slots), F32)
    packed = recs[...].astype(BF16)
    record[...] = packed
    chosen = (movev[...] == iota((8, slots), 0)) & (iota((8, slots), 1) < live)
    ones = chosen.astype(F32)
    scan_of = jnp.where(
        (iota((LANES, 2 * LANES), 0) < iota((LANES, 2 * LANES), 1))
        | (iota((LANES, 2 * LANES), 1) >= LANES),
        1.0,
        0.0,
    ).astype(BF16)
    carry = jnp.zeros((8, LANES), F32)
    ranks = []
    for block in range(slots // LANES):
        piece = ones[:, block * LANES : (block + 1) * LANES].astype(BF16)
        scanned = jnp.dot(piece, scan_of, preferred_element_type=F32)
        ranks.append(scanned[:, :LANES] + carry)
        carry = carry + scanned[:, LANES:]
    rank = jnp.where(chosen, jnp.concatenate(ranks, axis=1), -1.0).astype(I32)
    rank0[...] = rank[0:1]
    target = iota((HALF, slots), 0)
    placing = [
        jnp.where(rank[g : g + 1] == target, 1.0, 0.0).astype(BF16) for g in range(1, 5)
    ]
    lonrec[...] = nt(packed, jnp.concatenate(placing[:2], axis=0)).astype(BF16)
    latrec = nt(packed, jnp.concatenate(placing[2:], axis=0)).astype(BF16)
    number[0] = jnp.max(carry[0:1, :]).astype(I32)
    for comp in range(3):
        copies[2 * comp].wait()
        copies[2 * comp + 1].wait()

        def spread(k, _):
            for source, buffer in enumerate((low, high)):
                value = buffer[comp, k].astype(F32)
                for tile in range(tiles):
                    first = (source * tiles + tile) * 8 * stride + 3 * k + comp
                    strips[pl.ds(first, 8, stride=stride), :] = value[
                        :, tile * LANES : (tile + 1) * LANES
                    ]
            return 0

        lax.fori_loop(0, depth, spread, 0, unroll=15)
    odd = lax.rem(lax.axis_index("lat"), 2)
    for n, out in enumerate((q1, q2)):
        upper = odd if n == 0 else 1 - odd
        for tile in range(tiles):
            last = ((tiles + tile) * 8 + 7) * stride
            for line in range(2):
                first = jnp.where(upper == 1, (tile * 8 + line) * stride, last)
                at = (line * tiles + tile) * planes
                out[at : at + planes, :] = strips[pl.ds(first, planes), :].astype(BF16)
        out[2 * tiles * planes :, :] = latrec


def table_kernel(
    vel_hbm, record, rank0, number, first, last, seam, table, stay, index, vel, lines, wide, sems
):
    depth, rows, cols = vel.shape[1:]
    copies = [pltpu.make_async_copy(vel_hbm.at[c], vel.at[c], sems.at[c]) for c in range(3)]
    for copy in copies:
        copy.start()
    slots = record.shape[1]
    tiles = cols // LANES
    planes = up8(3 * depth)
    stride = odd_stride(depth)
    r, c = iota((REC, cols), 0), iota((REC, cols), 1)
    pick = (r == c) & (r < 2)
    pick = pick | ((r == 2) & (c == cols - 1)) | ((r == c - LANES + 4) & (r >= 3) & (r < 5))
    select = jnp.where(pick, 1.0, 0.0).astype(BF16)
    per = LANES // rows
    chunks = -(-depth // per)
    deep = up8(chunks)
    lane = iota((deep, LANES), 1)
    target = iota((LANES, slots), 0)
    packed = record[...]
    rank = rank0[...]
    for block in range(slots // LANES):
        where = jnp.where(rank - block * LANES == target, 1.0, 0.0).astype(BF16)
        out = nt(packed, where)
        lanes = slice(block * LANES, (block + 1) * LANES)
        for d, row in enumerate(decode(out)):
            stay[d : d + 1, lanes] = row
        stay[3:6, lanes] = out[9:12]
        stay[6:8, lanes] = out[12:14]
    i, j, k = (stay[n : n + 1, :].astype(I32) for n in (3, 4, 5))
    slot = iota((1, slots), 1)
    index[0:1, :] = ((i // LANES) * rows + j) * stride + 3 * k
    index[1:2, :] = (slot - i) & (LANES - 1)
    odd_one = (((i & (LANES - 1)) == LANES - 1) | (j == rows - 1)) & (slot < number[0])
    index[2:3, :] = odd_one.astype(I32)
    for comp in range(3):
        copies[comp].wait()
        got = nt(select, vel[comp].reshape(depth * rows, cols))
        for n in range(5):
            for q in range(chunks):
                size = min(LANES, depth * rows - q * LANES)
                lines[n * deep + q : n * deep + q + 1, 0:size] = got[
                    n : n + 1, q * LANES : q * LANES + size
                ]
        for m in range(per):

            def line(n, to):
                at = lines[n * deep : (n + 1) * deep, :]
                return pltpu.roll(at, (LANES + to - rows * m) % LANES, 1)

            values = (
                jnp.where(lane < HALF, line(0, 0), line(1, HALF)),
                line(2, 0),
                jnp.where(lane < HALF, line(3, 0), line(4, HALF)),
            )
            for n, value in enumerate(values):
                for q in range(0, deep, 8):
                    at = pl.ds(n * wide.shape[0] // 3 + 3 * (per * q + m) + comp, 8, stride=3 * per)
                    wide[at, :] = value[q : q + 8]
        def fill(k, _):
            value = vel[comp, k].astype(F32)
            for tile in range(tiles):
                for r in range(0, rows, 8):
                    at = pl.ds((tile * rows + r) * stride + 3 * k + comp, 8, stride=stride)
                    table[at, :] = value[r : r + 8, tile * LANES : (tile + 1) * LANES]
            return 0

        lax.fori_loop(0, depth, fill, 0, unroll=5)
    for n, out in enumerate((first, last, seam)):
        at = n * wide.shape[0] // 3
        out[...] = wide[at : at + planes, :]


def gather_kernel(stride, table, index, number, got, listed, found):
    lane = iota((8, LANES), 1)
    count = number[0]

    def block_of(b, n):
        acc = [jnp.zeros((8, LANES), F32)] * 4
        for p in range(LANES):
            s = b * LANES + p
            row = index[0, s]
            shift = index[1, s]
            low = pltpu.roll(table[pl.ds(row, 8), :], shift, 1)
            high = pltpu.roll(table[pl.ds(row + stride, 8), :], shift, 1)
            here = lane == p
            beside = lane == ((p + 1) % LANES)
            acc = [
                jnp.where(here, low, acc[0]),
                jnp.where(beside, low, acc[1]),
                jnp.where(here, high, acc[2]),
                jnp.where(beside, high, acc[3]),
            ]
            listed[n] = s
            n = n + index[2, s]
        got[0, b] = acc[0]
        got[1, b] = pltpu.roll(acc[1], LANES - 1, 1)
        got[2, b] = acc[2]
        got[3, b] = pltpu.roll(acc[3], LANES - 1, 1)
        return n

    found[0] = lax.fori_loop(0, (count + LANES - 1) // LANES, block_of, I32(0))


def side_kernel(first, last, lonrec, q1r, q2r, p1, p2):
    planes = first.shape[0]
    even_lat = lax.rem(lax.axis_index("lat"), 2) == 0
    odd_lon = lax.rem(lax.axis_index("lon"), 2)
    lane = iota((planes, LANES), 1)

    def strip(north, n):
        a = q1r[n * planes : (n + 1) * planes, :].astype(F32)
        b = q2r[n * planes : (n + 1) * planes, :].astype(F32)
        return jnp.where(even_lat == north, a, b)

    north0, north1, second0 = strip(True, 0), strip(True, 1), strip(True, 2)
    south0 = strip(False, 0)
    west = first[...]
    west = jnp.where(lane == 32, pltpu.roll(north0, 32, 1), west)
    west = jnp.where(lane == 33, pltpu.roll(second0, 33, 1), west)
    west = jnp.where(lane == 34, pltpu.roll(south0, 34, 1), west)
    west = jnp.where(lane == 35, pltpu.roll(north1, 36, 1), west)
    west = jnp.where(lane == 96, pltpu.roll(north0, 95, 1), west).astype(BF16)
    east = last[...]
    east = jnp.where(lane == 32, pltpu.roll(north1, 33, 1), east)
    east = jnp.where((lane == 33) | (lane == 34), pltpu.roll(north0, 33, 1), east).astype(BF16)
    p1[0:planes, :] = jnp.where(odd_lon == 1, west, east)
    p2[0:planes, :] = jnp.where(odd_lon == 1, east, west)
    p1[planes:, :] = lonrec[...]
    p2[planes:, :] = lonrec[...]


def final_kernel(
    rows, cols, lat_size,
    stay, number, got, listed, found, first, last, seam, q1, q2, q1r, q2r, p1r, p2r,
    new_off, new_cel, new_count, table, values_of, recs, idxv, idxs, isem,
):
    planes = first.shape[0]
    slots = stay.shape[1]
    values_of[...] = got[...]
    lat = lax.axis_index("lat")
    even_lat = lax.rem(lat, 2) == 0
    even_lon = lax.rem(lax.axis_index("lon"), 2) == 0
    top = lat == lat_size - 1
    both = 4 * planes

    def pick(flag, a, b, at, size):
        return jnp.where(flag, a[at : at + size, :], b[at : at + size, :]).astype(F32)

    def put(n, value):
        table[n * planes : (n + 1) * planes, :] = value

    for t in range(2):
        at = t * planes
        put(t, pick(even_lat, q2, q1, at, planes))
        put(2 + t, pick(even_lat, q1, q2, at, planes))
        put(4 + t, pick(even_lat, q1r, q2r, at, planes))
        put(6 + t, pick(even_lat, q1r, q2r, at + 2 * planes, planes))
        put(8 + t, pick(even_lat, q2r, q1r, at, planes))
    put(10, first[...])
    put(11, last[...])
    put(14, seam[...])
    put(12, pick(even_lon, p1r, p2r, 0, planes))
    put(13, pick(even_lon, p2r, p1r, 0, planes))
    lane = iota((8, LANES), 1)
    inside = iota((REC, LANES), 1) < HALF
    wrec = pick(even_lon, p2r, p1r, planes, REC)
    erec = pltpu.roll(pick(even_lon, p1r, p2r, planes, REC), HALF, 1)
    srec = pick(even_lat, q2r, q1r, both, REC)
    nrec = pick(even_lat, q1r, q2r, both, REC)
    nrec = jnp.where(top, nrec, pltpu.roll(nrec, HALF, 1))
    base = number[0]
    slot = iota((1, slots), 1)
    own = slot < base
    for n in range(8):
        recs[n : n + 1, :] = jnp.where(own, stay[n : n + 1, :], 0.0)
    group = jnp.zeros((1, slots), I32)
    stay_count = base
    for g, raw in enumerate((wrec, erec, srec, nrec)):
        raw = jnp.where(inside, raw, 0.0)
        count = jnp.sum(raw[12:13]).astype(I32)
        moved = pltpu.roll(raw, base & (LANES - 1), 1)
        values = decode(moved) + [moved[9:10], moved[10:11], moved[11:12]]
        mine = (slot >= base) & (slot < base + count)
        for b in range(slots // LANES):
            at = slice(b * LANES, (b + 1) * LANES)
            for n, row in enumerate(values):
                recs[n : n + 1, at] = jnp.where(mine[:, at], row, recs[n : n + 1, at])
        group = jnp.where(mine, g + 1, group)
        base = base + count
    fold = (group == 4) & top
    new_count[0, 0] = base
    i, j, k = (recs[n : n + 1, :].astype(I32) for n in (3, 4, 5))
    y0 = jnp.where(group == 3, -1, jnp.where((group == 4), rows, j))
    x0 = jnp.where(group == 1, -1, jnp.where(group == 2, cols, i))
    signs = []
    for n, (dj, di) in enumerate(((0, 0), (0, 1), (1, 0), (1, 1))):
        y = y0 + dj
        x = x0 + di

        def flat(strip, at):
            return strip * (planes * LANES) + at

        def row_at(strip, at):
            return flat(strip + at // LANES, at & (LANES - 1))

        inner = jnp.where(
            x < 0,
            flat(13, y),
            jnp.where(
                x == cols,
                flat(12, y),
                jnp.where(
                    x > cols,
                    flat(12, HALF + y),
                    jnp.where(
                        x == cols - 1,
                        flat(11, y),
                        jnp.where(
                            x == 0,
                            flat(10, y),
                            jnp.where(
                                x == LANES - 1,
                                flat(14, y),
                                jnp.where(
                                    x == LANES,
                                    flat(14, HALF + y),
                                    row_at(jnp.where(y == 0, 0, 2), x),
                                ),
                            ),
                        ),
                    ),
                ),
            ),
        )
        north = jnp.where(
            x < 0,
            flat(13, 32),
            jnp.where(x == cols, flat(12, 32), jnp.where(x > cols, flat(12, 96), row_at(4, x))),
        )
        u = cols - x
        folded = jnp.where(
            u < 0,
            flat(12, 35),
            jnp.where(u == cols, flat(13, 33), jnp.where(u > cols, flat(13, 34), row_at(4, u))),
        )
        second = jnp.where(x == cols, flat(12, 33), row_at(6, x))
        south = jnp.where(x == cols, flat(12, 34), row_at(8, x))
        where = jnp.where(
            y < 0,
            south,
            jnp.where(y > rows, second, jnp.where(y == rows, jnp.where(top, folded, north), inner)),
        )
        if dj == 0:
            across = jnp.where(x == cols, flat(13, 33), row_at(4, x))
            signs.append(jnp.ones((1, slots), F32))
        else:
            across = jnp.where(u == cols, flat(12, rows - 1), row_at(2, u))
            signs.append(jnp.where(fold | (top & (y == rows)), -1.0, 1.0))
        where = jnp.where(fold, across, where)
        idxv[n : n + 1, :] = where + 3 * LANES * k
    copy = pltpu.make_async_copy(idxv, idxs, isem)
    copy.start()
    copy.wait()

    def patch(chosen):
        values = []
        for s in chosen:
            for q in range(4):
                e = idxs[q, s]
                values.append(pltpu.roll(table[pl.ds(e // LANES, 8), :], (s - e) & (LANES - 1), 1))
        for s in chosen:
            mask = lane == (s & (LANES - 1))
            for q in range(4):
                pltpu.store(values_of.at[q, s // LANES], values.pop(0), mask=mask)

    def patch_listed(n, _):
        patch([listed[jnp.minimum(n * UNROLL + u, found[0] - 1)] for u in range(UNROLL)])
        return 0

    lax.fori_loop(0, (found[0] + UNROLL - 1) // UNROLL, patch_listed, 0)

    def patch_arrived(n, _):
        start = stay_count + n * UNROLL
        patch([jnp.minimum(start + u, slots - 1) for u in range(UNROLL)])
        return 0

    lax.fori_loop(0, (base - stay_count + UNROLL - 1) // UNROLL, patch_arrived, 0)
    below = iota((8, LANES), 0) < 3
    for b in range(slots // LANES):
        at = slice(b * LANES, (b + 1) * LANES)
        corner = [values_of[n, b] * signs[n][:, at] for n in range(4)]
        position = recs[0:3, at]

        def rounded(value):
            return value.astype(BF16).astype(F32)

        def sample(pos):
            pa, pb, pc = pos[0:1], pos[1:2], pos[2:3]
            near = jnp.where(below, rounded((1.0 - pb) * (1.0 - pc)), rounded((1.0 - pb) * pc))
            far = jnp.where(below, rounded(pb * (1.0 - pc)), rounded(pb * pc))
            left = near * corner[0] + far * corner[2]
            right = near * corner[1] + far * corner[3]
            mixed = (1.0 - pa) * left + pa * right
            return mixed[0:3] + mixed[3:6]

        middle = position + 0.5 * sample(position)
        moved = position + sample(middle)
        na, nb, nc = moved[0:1], moved[1:2], moved[2:3]
        g = group[:, at]
        f = fold[:, at]
        filled = slot[:, at] < base
        na = jnp.where(g == 1, na - 1.0, jnp.where(g == 2, na + 1.0, jnp.where(f, 1.0 - na, na)))
        north_b = jnp.where(f, 2.0 - nb, nb + 1.0)
        nb = jnp.where(g == 3, nb - 1.0, jnp.where(g == 4, north_b, nb))
        new_off[0, :, at] = jnp.where(filled, na, 0.0)
        new_off[1, :, at] = jnp.where(filled, nb, 0.0)
        new_off[2, :, at] = jnp.where(filled, nc, 0.0)
        ci, cj = i[:, at], j[:, at]
        ci = jnp.where(
            g == 1, 0, jnp.where(g == 2, cols - 1, jnp.where(f, cols - 1 - ci, ci))
        )
        cj = jnp.where(g == 3, 0, jnp.where(g == 4, rows - 1, cj))
        new_cel[0, :, at] = jnp.where(filled, ci, 0)
        new_cel[1, :, at] = jnp.where(filled, cj, 0)
        new_cel[2, :, at] = jnp.where(filled, k[:, at], 0)


def route(lon_size, lat_size, partner):
    pairs = []
    for p in range(lon_size):
        for r in range(lat_size):
            other = partner(p, r)
            if other is not None:
                pairs.append((p * lat_size + r, other[0] * lat_size + other[1]))
    return pairs


def shards(velocity, offsets, cells, counts, moves):
    depth, rows, cols = velocity.shape[1:]
    slots = offsets.shape[2]
    lon_size, lat_size = lax.axis_size("lon"), lax.axis_size("lat")
    axes = ("lon", "lat")
    planes = up8(3 * depth)
    stride = odd_stride(depth)
    tiles = cols // LANES
    high = 2 * tiles * planes + REC

    def send(x, partner):
        return lax.ppermute(x, axes, route(lon_size, lat_size, partner))

    def array(shape, dtype):
        return jax.ShapeDtypeStruct(shape, dtype)

    q1, q2, lonrec, record, rank0, number = pl.pallas_call(
        pack_kernel,
        out_shape=(
            array((high, LANES), BF16),
            array((high, LANES), BF16),
            array((REC, LANES), BF16),
            array((REC, slots), BF16),
            array((1, slots), I32),
            array((1,), I32),
        ),
        in_specs=[HBM, HBM, HBM, SMEM, HBM],
        out_specs=(VMEM, VMEM, VMEM, VMEM, VMEM, SMEM),
        scratch_shapes=[
            pltpu.VMEM((3, depth, 8, cols), BF16),
            pltpu.VMEM((3, depth, 8, cols), BF16),
            pltpu.VMEM((3, 1, slots), F32),
            pltpu.VMEM((3, 1, slots), I32),
            pltpu.VMEM((1, slots), I32),
            pltpu.VMEM((2 * tiles * 8 * stride, LANES), F32),
            pltpu.VMEM((REC, slots), F32),
            pltpu.SemaphoreType.DMA((2, 3)),
            pltpu.SemaphoreType.DMA((3,)),
        ],
        compiler_params=room(10),
        name="pack",
    )(*(pltpu.with_memory_space_constraint(x, pltpu.HBM) for x in (velocity, offsets, cells)), counts, pltpu.with_memory_space_constraint(moves, pltpu.HBM))

    q1r = send(q1, lambda p, r: (p, r ^ 1))

    def second(p, r):
        if r == lat_size - 1:
            return (lon_size - 1 - p, r)
        return None if r == 0 else (p, ((r + 1) ^ 1) - 1)

    q2r = send(q2, second)
    per = LANES // rows
    deep = up8(-(-depth // per))
    strips = tiles * rows + 1
    first, last, seam, table, stay, index = pl.pallas_call(
        table_kernel,
        out_shape=(
            array((planes, LANES), F32),
            array((planes, LANES), F32),
            array((planes, LANES), F32),
            array((strips * stride + 8, LANES), F32),
            array((8, slots), F32),
            array((3, slots), I32),
        ),
        in_specs=[HBM, VMEM, VMEM, SMEM],
        out_specs=(VMEM,) * 6,
        scratch_shapes=[
            pltpu.VMEM((3, depth, rows, cols), BF16),
            pltpu.VMEM((5 * deep, LANES), F32),
            pltpu.VMEM((9 * up8(per * deep), LANES), F32),
            pltpu.SemaphoreType.DMA((3,)),
        ],
        compiler_params=room(20),
        cost_estimate=pl.CostEstimate(flops=10**9, bytes_accessed=2 * velocity.size, transcendentals=0),
        name="table",
    )(pltpu.with_memory_space_constraint(velocity, pltpu.HBM), record, rank0, number)
    p1, p2 = pl.pallas_call(
        side_kernel,
        out_shape=(array((planes + REC, LANES), BF16), array((planes + REC, LANES), BF16)),
        in_specs=[VMEM] * 5,
        out_specs=(VMEM, VMEM),
        compiler_params=room(5),
        name="sides",
    )(first, last, lonrec, q1r, q2r)
    p2r = send(p2, lambda p, r: ((((p + 1) ^ 1) - 1) % lon_size, r))
    p1r = send(p1, lambda p, r: (p ^ 1, r))
    got, listed, found = pl.pallas_call(
        functools.partial(gather_kernel, stride),
        out_shape=(
            array((4, slots // LANES, 8, LANES), F32),
            array((slots + LANES,), I32),
            array((1,), I32),
        ),
        in_specs=[VMEM, SMEM, SMEM],
        out_specs=(VMEM, SMEM, SMEM),
        compiler_params=room(10),
        cost_estimate=pl.CostEstimate(flops=10**9, bytes_accessed=2 * velocity.size, transcendentals=0),
        name="gather",
    )(table, index, number)
    return pl.pallas_call(
        functools.partial(final_kernel, rows, cols, lat_size),
        out_shape=(
            array((3, 1, slots), F32),
            array((3, 1, slots), I32),
            array((1, 1), I32),
        ),
        in_specs=[VMEM, SMEM, VMEM, SMEM, SMEM] + [VMEM] * 9,
        out_specs=(VMEM, VMEM, SMEM),
        scratch_shapes=[
            pltpu.VMEM((15 * planes + 8, LANES), F32),
            pltpu.VMEM((4, slots // LANES, 8, LANES), F32),
            pltpu.VMEM((8, slots), F32),
            pltpu.VMEM((8, slots), I32),
            pltpu.SMEM((8, slots), I32),
            pltpu.SemaphoreType.DMA,
        ],
        compiler_params=room(8),
        name="final",
    )(stay, number, got, listed, found, first, last, seam, q1, q2, q1r, q2r, p1r, p2r)


def solution(mesh):
    placed = (
        P(None, None, "lat", "lon"),
        P(None, "lat", "lon"),
        P(None, "lat", "lon"),
        P("lat", "lon"),
        P("lat", "lon"),
    )
    return jax.shard_map(
        shards,
        mesh=mesh,
        in_specs=placed,
        out_specs=(P(None, "lat", "lon"), P(None, "lat", "lon"), P("lat", "lon")),
        check_vma=False,
    )
```

profile of v0, /device:TPU:3, one launch (start us, length us, event | category | flops | bytes accessed | tf_op | source)
XLA Modules:
  0.0 33.4 jit_solution(446393955243417770)
XLA Ops:
  1.3 2.5 %pack.1 = (bf16[944,128]{1,0:T(8,128)(2,1)S(1)}, bf16[944,128]{1,0:T(8,128)(2,1)S(1)}, bf16[16,128]{1,0:T(8,128)(2,1)S(1)}, bf16[16,768]{1,0:T(8,128)(2,1)S(1)}, s32[1,768]{1,0:T(1,128)S(1)}, /*index=5*/s32[1]{0:T(128)}) custom-call(bf16[3,75,32,256]{3,2,1,0:T(8,128)(2,1)} %vel_hbm.1, f32[3,1,768]{2,1,0:T(1,128)} %off.1, s32[3,1,768]{2,1,0:T(1,128)} %cel.1, ...), custom_call_target="tpu_custom_call" | custom-call | tf_op jit(solution)/shard_map/pack/pallas_call | solution.py:500
  3.8 0.7 %collective-permute-start = (bf16[944,128]{1,0:T(8,128)(2,1)S(1)}, bf16[944,128]{1,0:T(8,128)(2,1)S(1)}, u32[]{:S(2)}, u32[]{:S(2)}) collective-permute-start(bf16[944,128]{1,0:T(8,128)(2,1)S(1)} %get-tuple-element.32.q1), channel_id=1, source_target_pairs={{0,1},{1,0},{2,3},{3,2},{4,5},{5,4},{6,7},{7,6},{8,9},{9,8},{10,11... | collective-permute-start | bytes 725000 | tf_op jit(solution)/shard_map/ppermute | solution.py:495
  4.5 6.2 %collective-permute-start.1 = (bf16[944,128]{1,0:T(8,128)(2,1)S(1)}, bf16[944,128]{1,0:T(8,128)(2,1)S(1)}, u32[]{:S(2)}, u32[]{:S(2)}) collective-permute-start(bf16[944,128]{1,0:T(8,128)(2,1)S(1)} %get-tuple-element.33.q2), channel_id=1, source_target_pairs={{1,2},{2,1},{3,31},{5,6},{6,5},{7,27},{9,10},{10,9},{11,23},{13,14... | collective-permute-start | bytes 725000 | tf_op jit(solution)/shard_map/ppermute | solution.py:495
  10.7 4.1 %table.1 = (f32[232,128]{1,0:T(8,128)S(1)}, f32[232,128]{1,0:T(8,128)S(1)}, f32[232,128]{1,0:T(8,128)S(1)}, f32[15153,128]{1,0:T(8,128)S(1)}, f32[8,768]{1,0:T(8,128)S(1)}, /*index=5*/s32[3,768]{1,0:T(4,128)S(1)}) custom-call(bf16[3,75,32,256]{3,2,1,0:T(8,128)(2,1)} %vel_hbm.1, bf16[16,768]{1,0:T(8,128)(2,1)S(1)} %get-tuple-element.20.record, ...), custom_call_target="tpu_custom_call" | custom-call | flops 1000000000 | bytes 3686400 | tf_op jit(solution)/shard_map/table/pallas_call | solution.py:538
  14.9 0.0 collective-permute-done.q1r
  14.9 0.0 collective-permute-done.1.q2r
  14.9 0.2 sides.1
  15.1 0.6 %collective-permute-start.2 = (bf16[248,128]{1,0:T(8,128)(2,1)S(1)}, bf16[248,128]{1,0:T(8,128)(2,1)S(1)}, u32[]{:S(2)}, u32[]{:S(2)}) collective-permute-start(bf16[248,128]{1,0:T(8,128)(2,1)S(1)} %get-tuple-element.35), channel_id=1, source_target_pairs={{0,4},{1,5},{2,6},{3,7},{4,0},{5,1},{6,2},{7,3},{8,12},{9,13},{10,... | collective-permute-start | bytes 190472 | tf_op jit(solution)/shard_map/ppermute | solution.py:495
  15.7 3.3 %collective-permute-start.3 = (bf16[248,128]{1,0:T(8,128)(2,1)S(1)}, bf16[248,128]{1,0:T(8,128)(2,1)S(1)}, u32[]{:S(2)}, u32[]{:S(2)}) collective-permute-start(bf16[248,128]{1,0:T(8,128)(2,1)S(1)} %get-tuple-element.36), channel_id=1, source_target_pairs={{0,28},{1,29},{2,30},{3,31},{4,8},{5,9},{6,10},{7,11},{8,4},{9,5},... | collective-permute-start | bytes 190472 | tf_op jit(solution)/shard_map/ppermute | solution.py:495
  19.0 4.0 %gather.1 = (f32[4,6,8,128]{3,2,1,0:T(8,128)S(1)}, s32[896]{0:T(1024)S(1)}, s32[1]{0:T(128)}) custom-call(f32[15153,128]{1,0:T(8,128)S(1)} %get-tuple-element.24.table, s32[3,768]{1,0:T(4,128)S(1)} %get-tuple-element.25.index, s32[1]{0:T(128)} %get-tuple-element.22.number), custom_call_target="tpu_custom_call" | custom-call | flops 1000000000 | bytes 3686400 | tf_op jit(solution)/shard_map/gather/pallas_call | solution.py:570
  23.0 0.0 collective-permute-done.2.p1r
  23.1 0.0 collective-permute-done.3.p2r
  23.1 10.3 %final.1 = (f32[3,1,768]{2,1,0:T(1,128)}, s32[3,1,768]{2,1,0:T(1,128)}, s32[1,1]{1,0:T(1,128)}) custom-call(f32[8,768]{1,0:T(8,128)S(1)} %get-tuple-element.23.stay, s32[1]{0:T(128)} %get-tuple-element.22.number, f32[4,6,8,128]{3,2,1,0:T(8,128)S(1)} %get-tuple-element.26.got, s32[896]{0:T(1024)S(1)} %get-tuple-element.27.listed, s32[1]{0:T(128)} %get-tuple-element.28.found, ...), custom_call_target="tpu_custom_call" | custom-call | tf_op jit(solution)/shard_map/final/pallas_call | solution.py:583
Async XLA Ops:
  3.8 11.1 %collective-permute-start = (bf16[944,128]{1,0:T(8,128)(2,1)S(1)}, bf16[944,128]{1,0:T(8,128)(2,1)S(1)}, u32[]{:S(2)}, u32[]{:S(2)}) collective-permute-start(bf16[944,128]{1,0:T(8,128)(2,1)S(1)} %get-tuple-element.32.q1), channel_id=1, source_target_pairs={{0,1},{1,0},{2,3},{3,2},{4,5},{5,4},{6,7},{7,6},{8,9},{9,8},{10,11... | collective-permute-start | bytes 725000 | tf_op jit(solution)/shard_map/ppermute | solution.py:495
  4.5 10.3 %collective-permute-start.1 = (bf16[944,128]{1,0:T(8,128)(2,1)S(1)}, bf16[944,128]{1,0:T(8,128)(2,1)S(1)}, u32[]{:S(2)}, u32[]{:S(2)}) collective-permute-start(bf16[944,128]{1,0:T(8,128)(2,1)S(1)} %get-tuple-element.33.q2), channel_id=1, source_target_pairs={{1,2},{2,1},{3,31},{5,6},{6,5},{7,27},{9,10},{10,9},{11,23},{13,14... | collective-permute-start | bytes 725000 | tf_op jit(solution)/shard_map/ppermute | solution.py:495
  15.1 7.9 %collective-permute-start.2 = (bf16[248,128]{1,0:T(8,128)(2,1)S(1)}, bf16[248,128]{1,0:T(8,128)(2,1)S(1)}, u32[]{:S(2)}, u32[]{:S(2)}) collective-permute-start(bf16[248,128]{1,0:T(8,128)(2,1)S(1)} %get-tuple-element.35), channel_id=1, source_target_pairs={{0,4},{1,5},{2,6},{3,7},{4,0},{5,1},{6,2},{7,3},{8,12},{9,13},{10,... | collective-permute-start | bytes 190472 | tf_op jit(solution)/shard_map/ppermute | solution.py:495
  15.7 7.3 %collective-permute-start.3 = (bf16[248,128]{1,0:T(8,128)(2,1)S(1)}, bf16[248,128]{1,0:T(8,128)(2,1)S(1)}, u32[]{:S(2)}, u32[]{:S(2)}) collective-permute-start(bf16[248,128]{1,0:T(8,128)(2,1)S(1)} %get-tuple-element.36), channel_id=1, source_target_pairs={{0,28},{1,29},{2,30},{3,31},{4,8},{5,9},{6,10},{7,11},{8,4},{9,5},... | collective-permute-start | bytes 190472 | tf_op jit(solution)/shard_map/ppermute | solution.py:495
where the time goes:
time: 33.3 us; the launch traced here: 33.4 us
  Pallas kernels  21.2 us (64%)
  starting transfers between devices  10.8 us (32%)
  between operations  1.35 us (4%)
    ppermute x4, starting transfers between devices, send(): return lax.ppermute(x, axes, route(lon_size, lat_size, partner))  10.8 us
    pallas_call x1, Pallas kernels, shards(): pl.pallas_call(functools.partial(final_kernel, rows, cols, lat_size), out...  10.3 us
    pallas_call x1, Pallas kernels, shards(): pl.pallas_call(table_kernel, out_shape=(array((planes, LANES), F32), arra...  4.14 us
    pallas_call x1, Pallas kernels, shards(): pl.pallas_call(functools.partial(gather_kernel, stride), out_shape=(array...  4.03 us
    pallas_call x1, Pallas kernels, shards(): pl.pallas_call(pack_kernel, out_shape=(array((high, LANES), BF16), array(...  2.52 us
  transfers between devices with their start and end apart: 4, of which 0 were waited for; matrix products, arithmetic and copies ran while one was open for 0% of the time, Pallas kernels for 24%

commit v1 on v0

--- a/solution.py
+++ b/solution.py
@@ -11,7 +11,8 @@
 LANES = 128
 HALF = 64
 REC = 16
-UNROLL = 16
+UNROLL = 8
+SHIFT = 7
 F32, BF16, I32 = jnp.float32, jnp.bfloat16, jnp.int32
 VMEM = pl.BlockSpec(memory_space=pltpu.VMEM)
 SMEM = pl.BlockSpec(memory_space=pltpu.SMEM)
@@ -51,7 +52,7 @@
 
 
 def pack_kernel(
-    vel, off, cel, counts, moves, q1, q2, lonrec, record, rank0, number,
+    vel, off, cel, counts, moves, q1, q2, lonrec, record, rank0, total,
     low, high, offv, celv, movev, strips, recs, sems, small,
 ):
     depth, rows = vel.shape[1], vel.shape[2]
@@ -114,7 +115,7 @@
     ]
     lonrec[...] = nt(packed, jnp.concatenate(placing[:2], axis=0)).astype(BF16)
     latrec = nt(packed, jnp.concatenate(placing[2:], axis=0)).astype(BF16)
-    number[0] = jnp.max(carry[0:1, :]).astype(I32)
+    total[...] = carry[0:1, :].astype(I32)
     for comp in range(3):
         copies[2 * comp].wait()
         copies[2 * comp + 1].wait()
@@ -143,12 +144,9 @@
 
 
 def table_kernel(
-    vel_hbm, record, rank0, number, first, last, seam, table, stay, index, vel, lines, wide, sems
+    vel, record, rank0, total, first, last, seam, table, stay, index, lines, wide
 ):
     depth, rows, cols = vel.shape[1:]
-    copies = [pltpu.make_async_copy(vel_hbm.at[c], vel.at[c], sems.at[c]) for c in range(3)]
-    for copy in copies:
-        copy.start()
     slots = record.shape[1]
     tiles = cols // LANES
     planes = up8(3 * depth)
@@ -174,12 +172,12 @@
         stay[6:8, lanes] = out[12:14]
     i, j, k = (stay[n : n + 1, :].astype(I32) for n in (3, 4, 5))
     slot = iota((1, slots), 1)
-    index[0:1, :] = ((i // LANES) * rows + j) * stride + 3 * k
+    index[0:1, :] = ((i >> SHIFT) * rows + j) * stride + 3 * k
     index[1:2, :] = (slot - i) & (LANES - 1)
-    odd_one = (((i & (LANES - 1)) == LANES - 1) | (j == rows - 1)) & (slot < number[0])
+    odd_one = (((i & (LANES - 1)) == LANES - 1) | (j == rows - 1)) & (slot < jnp.tile(total[...], (1, slots // LANES)))
     index[2:3, :] = odd_one.astype(I32)
+    index[3:4, :] = jnp.tile(total[...], (1, slots // LANES))
     for comp in range(3):
-        copies[comp].wait()
         got = nt(select, vel[comp].reshape(depth * rows, cols))
         for n in range(5):
             for q in range(chunks):
@@ -216,9 +214,10 @@
         out[...] = wide[at : at + planes, :]
 
 
-def gather_kernel(stride, table, index, number, got, listed, found):
+def gather_kernel(stride, table, index, got, listed):
     lane = iota((8, LANES), 1)
-    count = number[0]
+    count = index[3, 0]
+    slots = index.shape[1]
 
     def block_of(b, n):
         acc = [jnp.zeros((8, LANES), F32)] * 4
@@ -244,7 +243,8 @@
         got[3, b] = pltpu.roll(acc[3], LANES - 1, 1)
         return n
 
-    found[0] = lax.fori_loop(0, (count + LANES - 1) // LANES, block_of, I32(0))
+    listed[slots + 8] = lax.fori_loop(0, (count + LANES - 1) >> SHIFT, block_of, I32(0))
+    listed[slots + 9] = count
 
 
 def side_kernel(first, last, lonrec, q1r, q2r, p1, p2):
@@ -275,109 +275,27 @@
     p2[planes:, :] = lonrec[...]
 
 
-def final_kernel(
-    rows, cols, lat_size,
-    stay, number, got, listed, found, first, last, seam, q1, q2, q1r, q2r, p1r, p2r,
-    new_off, new_cel, new_count, table, values_of, recs, idxv, idxs, isem,
-):
-    planes = first.shape[0]
-    slots = stay.shape[1]
-    values_of[...] = got[...]
-    lat = lax.axis_index("lat")
-    even_lat = lax.rem(lat, 2) == 0
-    even_lon = lax.rem(lax.axis_index("lon"), 2) == 0
-    top = lat == lat_size - 1
-    both = 4 * planes
-
-    def pick(flag, a, b, at, size):
-        return jnp.where(flag, a[at : at + size, :], b[at : at + size, :]).astype(F32)
-
-    def put(n, value):
-        table[n * planes : (n + 1) * planes, :] = value
-
-    for t in range(2):
-        at = t * planes
-        put(t, pick(even_lat, q2, q1, at, planes))
-        put(2 + t, pick(even_lat, q1, q2, at, planes))
-        put(4 + t, pick(even_lat, q1r, q2r, at, planes))
-        put(6 + t, pick(even_lat, q1r, q2r, at + 2 * planes, planes))
-        put(8 + t, pick(even_lat, q2r, q1r, at, planes))
-    put(10, first[...])
-    put(11, last[...])
-    put(14, seam[...])
-    put(12, pick(even_lon, p1r, p2r, 0, planes))
-    put(13, pick(even_lon, p2r, p1r, 0, planes))
-    lane = iota((8, LANES), 1)
-    inside = iota((REC, LANES), 1) < HALF
-    wrec = pick(even_lon, p2r, p1r, planes, REC)
-    erec = pltpu.roll(pick(even_lon, p1r, p2r, planes, REC), HALF, 1)
-    srec = pick(even_lat, q2r, q1r, both, REC)
-    nrec = pick(even_lat, q1r, q2r, both, REC)
-    nrec = jnp.where(top, nrec, pltpu.roll(nrec, HALF, 1))
-    base = number[0]
-    slot = iota((1, slots), 1)
-    own = slot < base
-    for n in range(8):
-        recs[n : n + 1, :] = jnp.where(own, stay[n : n + 1, :], 0.0)
-    group = jnp.zeros((1, slots), I32)
-    stay_count = base
-    for g, raw in enumerate((wrec, erec, srec, nrec)):
-        raw = jnp.where(inside, raw, 0.0)
-        count = jnp.sum(raw[12:13]).astype(I32)
-        moved = pltpu.roll(raw, base & (LANES - 1), 1)
-        values = decode(moved) + [moved[9:10], moved[10:11], moved[11:12]]
-        mine = (slot >= base) & (slot < base + count)
-        for b in range(slots // LANES):
-            at = slice(b * LANES, (b + 1) * LANES)
-            for n, row in enumerate(values):
-                recs[n : n + 1, at] = jnp.where(mine[:, at], row, recs[n : n + 1, at])
-        group = jnp.where(mine, g + 1, group)
-        base = base + count
+def places(rows, cols, planes, group, top, y0, x0, k):
     fold = (group == 4) & top
-    new_count[0, 0] = base
-    i, j, k = (recs[n : n + 1, :].astype(I32) for n in (3, 4, 5))
-    y0 = jnp.where(group == 3, -1, jnp.where((group == 4), rows, j))
-    x0 = jnp.where(group == 1, -1, jnp.where(group == 2, cols, i))
-    signs = []
-    for n, (dj, di) in enumerate(((0, 0), (0, 1), (1, 0), (1, 1))):
+    found, signs = [], []
+
+    def flat(strip, at):
+        return strip * (planes * LANES) + at
+
+    def row_at(strip, at):
+        return flat(strip + (at >> SHIFT), at & (LANES - 1))
+
+    for dj, di in ((0, 0), (0, 1), (1, 0), (1, 1)):
         y = y0 + dj
         x = x0 + di
-
-        def flat(strip, at):
-            return strip * (planes * LANES) + at
-
-        def row_at(strip, at):
-            return flat(strip + at // LANES, at & (LANES - 1))
-
-        inner = jnp.where(
-            x < 0,
-            flat(13, y),
-            jnp.where(
-                x == cols,
-                flat(12, y),
-                jnp.where(
-                    x > cols,
-                    flat(12, HALF + y),
-                    jnp.where(
-                        x == cols - 1,
-                        flat(11, y),
-                        jnp.where(
-                            x == 0,
-                            flat(10, y),
-                            jnp.where(
-                                x == LANES - 1,
-                                flat(14, y),
-                                jnp.where(
-                                    x == LANES,
-                                    flat(14, HALF + y),
-                                    row_at(jnp.where(y == 0, 0, 2), x),
-                                ),
-                            ),
-                        ),
-                    ),
-                ),
-            ),
-        )
+        inner = row_at(jnp.where(y == 0, 0, 2), x)
+        inner = jnp.where(x == LANES - 1, flat(14, y), inner)
+        inner = jnp.where(x == LANES, flat(14, HALF + y), inner)
+        inner = jnp.where(x == 0, flat(10, y), inner)
+        inner = jnp.where(x == cols - 1, flat(11, y), inner)
+        inner = jnp.where(x > cols, flat(12, HALF + y), inner)
+        inner = jnp.where(x == cols, flat(12, y), inner)
+        inner = jnp.where(x < 0, flat(13, y), inner)
         north = jnp.where(
             x < 0,
             flat(13, 32),
@@ -398,44 +316,133 @@
         )
         if dj == 0:
             across = jnp.where(x == cols, flat(13, 33), row_at(4, x))
-            signs.append(jnp.ones((1, slots), F32))
+            signs.append(jnp.ones(x0.shape, F32))
         else:
             across = jnp.where(u == cols, flat(12, rows - 1), row_at(2, u))
-            signs.append(jnp.where(fold | (top & (y == rows)), -1.0, 1.0))
-        where = jnp.where(fold, across, where)
-        idxv[n : n + 1, :] = where + 3 * LANES * k
-    copy = pltpu.make_async_copy(idxv, idxs, isem)
+            signs.append(jnp.where(top & (fold | (y == rows)), -1.0, 1.0))
+        found.append(jnp.where(fold, across, where) + 3 * LANES * k)
+    return found, signs
+
+
+def final_kernel(
+    rows, cols, lat_size,
+    stay, got, listed_any, first, last, seam, q1, q2, q1r, q2r, p1r, p2r,
+    new_off, new_cel, new_count,
+    table, values_of, packed, idxv, idxs, idxlv, idxl, listed, isem,
+):
+    planes = first.shape[0]
+    slots = stay.shape[1]
+    lat = lax.axis_index("lat")
+    even_lat = lax.rem(lat, 2) == 0
+    even_lon = lax.rem(lax.axis_index("lon"), 2) == 0
+    top = lat == lat_size - 1
+    both = 4 * planes
+
+    def pick(flag, a, b, at, size):
+        return jnp.where(flag, a[at : at + size, :], b[at : at + size, :]).astype(F32)
+
+    slot = iota((1, slots), 1)
+    copy_list = pltpu.make_async_copy(listed_any, listed, isem.at[2])
+    copy_list.start()
+    blocks = [slice(b * LANES, (b + 1) * LANES) for b in range(slots // LANES)]
+    packed[...] = jnp.zeros(packed.shape, F32)
+    for n in range(3):
+        for b, at in enumerate(blocks):
+            packed[8 * n + b : 8 * n + b + 1, :] = stay[3 + n : 4 + n, at]
+    here = [packed[8 * n : 8 * n + 8, :].astype(I32) for n in range(3)]
+    e, stay_signs = places(
+        rows, cols, planes, jnp.zeros((8, LANES), I32), top, here[1], here[0], here[2]
+    )
+    for q in range(4):
+        idxlv[8 * q : 8 * q + 8, :] = e[q]
+    copy_listed = pltpu.make_async_copy(idxlv, idxl, isem.at[0])
+    copy_listed.start()
+    inside = iota((REC, LANES), 1) < HALF
+    wrec = pick(even_lon, p2r, p1r, planes, REC)
+    erec = pltpu.roll(pick(even_lon, p1r, p2r, planes, REC), HALF, 1)
+    srec = pick(even_lat, q2r, q1r, both, REC)
+    nrec = pick(even_lat, q1r, q2r, both, REC)
+    nrec = jnp.where(top, nrec, pltpu.roll(nrec, HALF, 1))
+    groups = []
+    for g, raw in enumerate((wrec, erec, srec, nrec)):
+        raw = jnp.where(inside, raw, 0.0)
+        count = jnp.sum(raw[12:13]).astype(I32)
+        i, j, k = (raw[n : n + 1].astype(I32) for n in (9, 10, 11))
+        y0 = (j, j, jnp.full_like(j, -1), jnp.full_like(j, rows))[g]
+        x0 = (jnp.full_like(i, -1), jnp.full_like(i, cols), i, i)[g]
+        e, signs = places(rows, cols, planes, jnp.full_like(i, g + 1), top, y0, x0, k)
+        for q in range(4):
+            row = 4 * g + q
+            idxv[row : row + 1, :] = e[q]
+        groups.append((raw, count, signs))
+    copy = pltpu.make_async_copy(idxv, idxs, isem.at[1])
     copy.start()
-    copy.wait()
-
-    def patch(chosen):
+    values_of[...] = got[...]
+
+    def put(n, value):
+        table[n * planes : (n + 1) * planes, :] = value
+
+    for t in range(2):
+        at = t * planes
+        put(t, pick(even_lat, q2, q1, at, planes))
+        put(2 + t, pick(even_lat, q1, q2, at, planes))
+        put(4 + t, pick(even_lat, q1r, q2r, at, planes))
+        put(6 + t, pick(even_lat, q1r, q2r, at + 2 * planes, planes))
+        put(8 + t, pick(even_lat, q2r, q1r, at, planes))
+    put(10, first[...])
+    put(11, last[...])
+    put(12, pick(even_lon, p1r, p2r, 0, planes))
+    put(13, pick(even_lon, p2r, p1r, 0, planes))
+    put(14, seam[...])
+    lane = iota((8, LANES), 1)
+    copy_listed.wait()
+    copy_list.wait()
+    found = listed[slots + 8]
+
+    def patch_listed(n, _):
+        chosen = [listed[jnp.minimum(n * UNROLL + u, found - 1)] for u in range(UNROLL)]
         values = []
         for s in chosen:
             for q in range(4):
-                e = idxs[q, s]
-                values.append(pltpu.roll(table[pl.ds(e // LANES, 8), :], (s - e) & (LANES - 1), 1))
+                e = idxl[8 * q + (s >> SHIFT), s & (LANES - 1)]
+                values.append(pltpu.roll(table[pl.ds(e >> SHIFT, 8), :], (s - e) & (LANES - 1), 1))
         for s in chosen:
             mask = lane == (s & (LANES - 1))
             for q in range(4):
-                pltpu.store(values_of.at[q, s // LANES], values.pop(0), mask=mask)
-
-    def patch_listed(n, _):
-        patch([listed[jnp.minimum(n * UNROLL + u, found[0] - 1)] for u in range(UNROLL)])
+                pltpu.store(values_of.at[q, s >> SHIFT], values.pop(0), mask=mask)
         return 0
 
-    lax.fori_loop(0, (found[0] + UNROLL - 1) // UNROLL, patch_listed, 0)
-
-    def patch_arrived(n, _):
-        start = stay_count + n * UNROLL
-        patch([jnp.minimum(start + u, slots - 1) for u in range(UNROLL)])
-        return 0
-
-    lax.fori_loop(0, (base - stay_count + UNROLL - 1) // UNROLL, patch_arrived, 0)
+    lax.fori_loop(0, lax.div(found + (UNROLL - 1), UNROLL), patch_listed, 0)
+    copy.wait()
+    base = listed[slots + 9]
+    own = slot < base
+    corner = [
+        [values_of[n, b] * stay_signs[n][b : b + 1] for n in range(4)] for b in range(len(blocks))
+    ]
+    kept = [[jnp.where(own[:, at], stay[n : n + 1, at], 0.0) for n in range(6)] for at in blocks]
+    group = jnp.zeros((1, slots), I32)
+    for g, (raw, count, signs) in enumerate(groups):
+        acc = []
+        for q in range(4):
+            total = jnp.zeros((8, LANES), F32)
+            for t in range(CAP):
+                e = idxs[4 * g + q, t]
+                value = pltpu.roll(table[pl.ds(e >> SHIFT, 8), :], (t - e) & (LANES - 1), 1)
+                total = jnp.where(lane == t, value, total)
+            acc.append(pltpu.roll(total * signs[q], base & (LANES - 1), 1))
+        moved = pltpu.roll(raw, base & (LANES - 1), 1)
+        values = decode(moved) + [moved[9:10], moved[10:11], moved[11:12]]
+        mine = (slot >= base) & (slot < base + count)
+        for b, at in enumerate(blocks):
+            kept[b] = [jnp.where(mine[:, at], x, y) for x, y in zip(values, kept[b])]
+            corner[b] = [jnp.where(mine[:, at], x, y) for x, y in zip(acc, corner[b])]
+        group = jnp.where(mine, g + 1, group)
+        base = base + count
+    fold = (group == 4) & top
+    new_count[0, 0] = base
     below = iota((8, LANES), 0) < 3
-    for b in range(slots // LANES):
-        at = slice(b * LANES, (b + 1) * LANES)
-        corner = [values_of[n, b] * signs[n][:, at] for n in range(4)]
-        position = recs[0:3, at]
+    for b, at in enumerate(blocks):
+        position = jnp.concatenate(kept[b][:3], axis=0)
 
         def rounded(value):
             return value.astype(BF16).astype(F32)
@@ -444,8 +451,8 @@
             pa, pb, pc = pos[0:1], pos[1:2], pos[2:3]
             near = jnp.where(below, rounded((1.0 - pb) * (1.0 - pc)), rounded((1.0 - pb) * pc))
             far = jnp.where(below, rounded(pb * (1.0 - pc)), rounded(pb * pc))
-            left = near * corner[0] + far * corner[2]
-            right = near * corner[1] + far * corner[3]
+            left = near * corner[b][0] + far * corner[b][2]
+            right = near * corner[b][1] + far * corner[b][3]
             mixed = (1.0 - pa) * left + pa * right
             return mixed[0:3] + mixed[3:6]
 
@@ -461,14 +468,14 @@
         new_off[0, :, at] = jnp.where(filled, na, 0.0)
         new_off[1, :, at] = jnp.where(filled, nb, 0.0)
         new_off[2, :, at] = jnp.where(filled, nc, 0.0)
-        ci, cj = i[:, at], j[:, at]
+        ci, cj, ck = (row.astype(I32) for row in kept[b][3:])
         ci = jnp.where(
             g == 1, 0, jnp.where(g == 2, cols - 1, jnp.where(f, cols - 1 - ci, ci))
         )
         cj = jnp.where(g == 3, 0, jnp.where(g == 4, rows - 1, cj))
         new_cel[0, :, at] = jnp.where(filled, ci, 0)
         new_cel[1, :, at] = jnp.where(filled, cj, 0)
-        new_cel[2, :, at] = jnp.where(filled, k[:, at], 0)
+        new_cel[2, :, at] = jnp.where(filled, ck, 0)
 
 
 def route(lon_size, lat_size, partner):
@@ -497,7 +504,7 @@
     def array(shape, dtype):
         return jax.ShapeDtypeStruct(shape, dtype)
 
-    q1, q2, lonrec, record, rank0, number = pl.pallas_call(
+    q1, q2, lonrec, record, rank0, total = pl.pallas_call(
         pack_kernel,
         out_shape=(
             array((high, LANES), BF16),
@@ -505,10 +512,10 @@
             array((REC, LANES), BF16),
             array((REC, slots), BF16),
             array((1, slots), I32),
-            array((1,), I32),
+            array((1, LANES), I32),
         ),
         in_specs=[HBM, HBM, HBM, SMEM, HBM],
-        out_specs=(VMEM, VMEM, VMEM, VMEM, VMEM, SMEM),
+        out_specs=(VMEM,) * 6,
         scratch_shapes=[
             pltpu.VMEM((3, depth, 8, cols), BF16),
             pltpu.VMEM((3, depth, 8, cols), BF16),
@@ -543,20 +550,18 @@
             array((planes, LANES), F32),
             array((strips * stride + 8, LANES), F32),
             array((8, slots), F32),
-            array((3, slots), I32),
+            array((4, slots), I32),
         ),
-        in_specs=[HBM, VMEM, VMEM, SMEM],
+        in_specs=[VMEM] * 4,
         out_specs=(VMEM,) * 6,
         scratch_shapes=[
-            pltpu.VMEM((3, depth, rows, cols), BF16),
             pltpu.VMEM((5 * deep, LANES), F32),
             pltpu.VMEM((9 * up8(per * deep), LANES), F32),
-            pltpu.SemaphoreType.DMA((3,)),
         ],
         compiler_params=room(20),
         cost_estimate=pl.CostEstimate(flops=10**9, bytes_accessed=2 * velocity.size, transcendentals=0),
         name="table",
-    )(pltpu.with_memory_space_constraint(velocity, pltpu.HBM), record, rank0, number)
+    )(pltpu.with_memory_space_constraint(velocity, pltpu.VMEM), record, rank0, total)
     p1, p2 = pl.pallas_call(
         side_kernel,
         out_shape=(array((planes + REC, LANES), BF16), array((planes + REC, LANES), BF16)),
@@ -567,19 +572,18 @@
     )(first, last, lonrec, q1r, q2r)
     p2r = send(p2, lambda p, r: ((((p + 1) ^ 1) - 1) % lon_size, r))
     p1r = send(p1, lambda p, r: (p ^ 1, r))
-    got, listed, found = pl.pallas_call(
+    got, listed = pl.pallas_call(
         functools.partial(gather_kernel, stride),
         out_shape=(
             array((4, slots // LANES, 8, LANES), F32),
             array((slots + LANES,), I32),
-            array((1,), I32),
         ),
-        in_specs=[VMEM, SMEM, SMEM],
-        out_specs=(VMEM, SMEM, SMEM),
+        in_specs=[VMEM, SMEM],
+        out_specs=(VMEM, SMEM),
         compiler_params=room(10),
         cost_estimate=pl.CostEstimate(flops=10**9, bytes_accessed=2 * velocity.size, transcendentals=0),
         name="gather",
-    )(table, index, number)
+    )(table, index)
     return pl.pallas_call(
         functools.partial(final_kernel, rows, cols, lat_size),
         out_shape=(
@@ -587,19 +591,22 @@
             array((3, 1, slots), I32),
             array((1, 1), I32),
         ),
-        in_specs=[VMEM, SMEM, VMEM, SMEM, SMEM] + [VMEM] * 9,
+        in_specs=[VMEM, VMEM, pl.BlockSpec(memory_space=pl.ANY)] + [VMEM] * 9,
         out_specs=(VMEM, VMEM, SMEM),
         scratch_shapes=[
             pltpu.VMEM((15 * planes + 8, LANES), F32),
             pltpu.VMEM((4, slots // LANES, 8, LANES), F32),
-            pltpu.VMEM((8, slots), F32),
-            pltpu.VMEM((8, slots), I32),
-            pltpu.SMEM((8, slots), I32),
-            pltpu.SemaphoreType.DMA,
+            pltpu.VMEM((24, LANES), F32),
+            pltpu.VMEM((16, LANES), I32),
+            pltpu.SMEM((16, LANES), I32),
+            pltpu.VMEM((32, LANES), I32),
+            pltpu.SMEM((32, LANES), I32),
+            pltpu.SMEM((slots + LANES,), I32),
+            pltpu.SemaphoreType.DMA((3,)),
         ],
         compiler_params=room(8),
         name="final",
-    )(stay, number, got, listed, found, first, last, seam, q1, q2, q1r, q2r, p1r, p2r)
+    )(stay, got, listed, first, last, seam, q1, q2, q1r, q2r, p1r, p2r)
 
 
 def solution(mesh):

time: 33.3 us -> 26.2 us (0.79)
  Pallas kernels: 21.2 us -> 12.9 us
  local copies, waits for them, and re-layouts: 0 us -> 2.04 us
  starting transfers between devices: 10.8 us -> 10.3 us
    pallas_call x1, Pallas kernels: 10.3 us -> 3.85 us  [shards(): pl.pallas_call(functools.partial(final_kernel, rows, cols, lat_size), out...]
    unnamed x0 -> x2, local copies, waits for them, and re-layouts: none -> 2.04 us
    pallas_call x1, Pallas kernels: 4.14 us -> 2.58 us  [shards(): pl.pallas_call(table_kernel, out_shape=(array((planes, LANES), F32), arra...]
    ppermute x4, starting transfers between devices: 10.8 us -> 10.3 us  [send(): return lax.ppermute(x, axes, route(lon_size, lat_size, partner))]
    pallas_call x1, Pallas kernels: 2.52 us -> 2.06 us  [shards(): pl.pallas_call(pack_kernel, out_shape=(array((high, LANES), BF16), array(...]
  transfers between devices with their start and end apart: 4 -> 4, of which waited for: 0 -> 0; matrix products, arithmetic and copies ran while one was open for 0% -> 0% of each run, Pallas kernels for 24% -> 25%
where the time goes in v1:
time: 26.2 us; the launch traced here: 26.6 us
  Pallas kernels  12.9 us (49%)
  starting transfers between devices  10.3 us (39%)
  local copies, waits for them, and re-layouts  2.04 us (8%)
  between operations  1.36 us (5%)
    ppermute x4, starting transfers between devices, send(): return lax.ppermute(x, axes, route(lon_size, lat_size, partner))  10.3 us
    pallas_call x1, Pallas kernels, shards(): pl.pallas_call(functools.partial(gather_kernel, stride), out_shape=(array...  4.16 us
    pallas_call x1, Pallas kernels, shards(): pl.pallas_call(functools.partial(final_kernel, rows, cols, lat_size), out...  3.85 us
    pallas_call x1, Pallas kernels, shards(): pl.pallas_call(table_kernel, out_shape=(array((planes, LANES), F32), arra...  2.58 us
    pallas_call x1, Pallas kernels, shards(): pl.pallas_call(pack_kernel, out_shape=(array((high, LANES), BF16), array(...  2.06 us
    unnamed x2, local copies, waits for them, and re-layouts  2.04 us
  transfers between devices with their start and end apart: 4, of which 0 were waited for; matrix products, arithmetic and copies ran while one was open for 0% of the time, Pallas kernels for 25%

profile of v1, /device:TPU:3, one launch (start us, length us, event | category | flops | bytes accessed | tf_op | source)
XLA Modules:
  0.0 26.6 jit_solution(2731056614911270887)
XLA Ops:
  1.3 2.1 %pack.1 = (bf16[944,128]{1,0:T(8,128)(2,1)S(1)}, bf16[944,128]{1,0:T(8,128)(2,1)S(1)}, bf16[16,128]{1,0:T(8,128)(2,1)S(1)}, bf16[16,768]{1,0:T(8,128)(2,1)S(1)},...) custom-call(bf16[3,75,32,256]{3,2,1,0:T(8,128)(2,1)} %vel.3, f32[3,1,768]{2,1,0:T(1,128)} %off.1, s32[3,1,768]{2,1,0:T(1,128)} %cel.1, ...), custom_call_target="tpu_custom_call" | custom-call | tf_op jit(solution)/shard_map/pack/pallas_call | solution.py:507
  3.3 0.7 %collective-permute-start = (bf16[944,128]{1,0:T(8,128)(2,1)S(1)}, bf16[944,128]{1,0:T(8,128)(2,1)S(1)}, u32[]{:S(2)}, u32[]{:S(2)}) collective-permute-start(bf16[944,128]{1,0:T(8,128)(2,1)S(1)} %get-tuple-element.30.q1), channel_id=1, source_target_pairs={{0,1},{1,0},{2,3},{3,2},{4,5},{5,4},{6,7},{7,6},{8,9},{9,8},{10,11... | collective-permute-start | bytes 725000 | tf_op jit(solution)/shard_map/ppermute | solution.py:502
  4.1 6.2 %collective-permute-start.1 = (bf16[944,128]{1,0:T(8,128)(2,1)S(1)}, bf16[944,128]{1,0:T(8,128)(2,1)S(1)}, u32[]{:S(2)}, u32[]{:S(2)}) collective-permute-start(bf16[944,128]{1,0:T(8,128)(2,1)S(1)} %get-tuple-element.31.q2), channel_id=1, source_target_pairs={{1,2},{2,1},{3,31},{5,6},{6,5},{7,27},{9,10},{10,9},{11,23},{13,14... | collective-permute-start | bytes 725000 | tf_op jit(solution)/shard_map/ppermute | solution.py:502
  10.3 0.0 copy-start
  10.3 2.0 %copy-done = bf16[3,75,32,256]{3,2,1,0:T(8,128)(2,1)S(1)} copy-done((bf16[3,75,32,256]{3,2,1,0:T(8,128)(2,1)S(1)}, bf16[3,75,32,256]{3,2,1,0:T(8,128)(2,1)}, u32[]{:S(2)}) %copy-start) | copy-done | bytes 3686424
  12.3 2.6 %table.1 = (f32[232,128]{1,0:T(8,128)S(1)}, f32[232,128]{1,0:T(8,128)S(1)}, f32[232,128]{1,0:T(8,128)S(1)}, f32[15153,128]{1,0:T(8,128)S(1)}, f32[8,768]{1,0:T(8,128)S(1)}, /*index=5*/s32[4,768]{1,0:T(4,128)S(1)}) custom-call(bf16[3,75,32,256]{3,2,1,0:T(8,128)(2,1)S(1)} %copy-done, bf16[16,768]{1,0:T(8,128)(2,1)S(1)} %get-tuple-element.19.record, ...), custom_call_target="tpu_custom_call" | custom-call | flops 1000000000 | bytes 3686400 | tf_op jit(solution)/shard_map/table/pallas_call | solution.py:545
  14.9 0.0 collective-permute-done.q1r
  14.9 0.0 collective-permute-done.1.q2r
  14.9 0.2 sides.1
  15.1 0.3 %collective-permute-start.2 = (bf16[248,128]{1,0:T(8,128)(2,1)S(1)}, bf16[248,128]{1,0:T(8,128)(2,1)S(1)}, u32[]{:S(2)}, u32[]{:S(2)}) collective-permute-start(bf16[248,128]{1,0:T(8,128)(2,1)S(1)} %get-tuple-element.33), channel_id=1, source_target_pairs={{0,4},{1,5},{2,6},{3,7},{4,0},{5,1},{6,2},{7,3},{8,12},{9,13},{10,... | collective-permute-start | bytes 190472 | tf_op jit(solution)/shard_map/ppermute | solution.py:502
  15.4 3.1 %collective-permute-start.3 = (bf16[248,128]{1,0:T(8,128)(2,1)S(1)}, bf16[248,128]{1,0:T(8,128)(2,1)S(1)}, u32[]{:S(2)}, u32[]{:S(2)}) collective-permute-start(bf16[248,128]{1,0:T(8,128)(2,1)S(1)} %get-tuple-element.34), channel_id=1, source_target_pairs={{0,28},{1,29},{2,30},{3,31},{4,8},{5,9},{6,10},{7,11},{8,4},{9,5},... | collective-permute-start | bytes 190472 | tf_op jit(solution)/shard_map/ppermute | solution.py:502
  18.6 4.2 %gather.1 = (f32[4,6,8,128]{3,2,1,0:T(8,128)S(1)}, s32[896]{0:T(1024)S(1)}) custom-call(f32[15153,128]{1,0:T(8,128)S(1)} %get-tuple-element.23.table, s32[4,768]{1,0:T(4,128)S(1)} %get-tuple-element.24.index), custom_call_target="tpu_custom_call" | custom-call | flops 1000000000 | bytes 3686400 | tf_op jit(solution)/shard_map/gather/pallas_call | solution.py:575
  22.7 0.0 collective-permute-done.2.p1r
  22.7 0.0 collective-permute-done.3.p2r
  22.7 3.8 %final.1 = (f32[3,1,768]{2,1,0:T(1,128)}, s32[3,1,768]{2,1,0:T(1,128)}, s32[1,1]{1,0:T(1,128)}) custom-call(f32[8,768]{1,0:T(8,128)S(1)} %get-tuple-element.22.stay, f32[4,6,8,128]{3,2,1,0:T(8,128)S(1)} %get-tuple-element.25.got, s32[896]{0:T(1024)S(1)} %get-tuple-element.26.listed_any, f32[232,128]{1,0:T(8,128)S(1)} %get-tuple-element.27.first, ...), custom_call_target="tpu_custom_call" | custom-call | tf_op jit(solution)/shard_map/final/pallas_call | solution.py:587
Async XLA Ops:
  3.3 11.6 %collective-permute-start = (bf16[944,128]{1,0:T(8,128)(2,1)S(1)}, bf16[944,128]{1,0:T(8,128)(2,1)S(1)}, u32[]{:S(2)}, u32[]{:S(2)}) collective-permute-start(bf16[944,128]{1,0:T(8,128)(2,1)S(1)} %get-tuple-element.30.q1), channel_id=1, source_target_pairs={{0,1},{1,0},{2,3},{3,2},{4,5},{5,4},{6,7},{7,6},{8,9},{9,8},{10,11... | collective-permute-start | bytes 725000 | tf_op jit(solution)/shard_map/ppermute | solution.py:502
  4.1 10.8 %collective-permute-start.1 = (bf16[944,128]{1,0:T(8,128)(2,1)S(1)}, bf16[944,128]{1,0:T(8,128)(2,1)S(1)}, u32[]{:S(2)}, u32[]{:S(2)}) collective-permute-start(bf16[944,128]{1,0:T(8,128)(2,1)S(1)} %get-tuple-element.31.q2), channel_id=1, source_target_pairs={{1,2},{2,1},{3,31},{5,6},{6,5},{7,27},{9,10},{10,9},{11,23},{13,14... | collective-permute-start | bytes 725000 | tf_op jit(solution)/shard_map/ppermute | solution.py:502
  10.3 2.0 %copy-start = (bf16[3,75,32,256]{3,2,1,0:T(8,128)(2,1)S(1)}, bf16[3,75,32,256]{3,2,1,0:T(8,128)(2,1)}, u32[]{:S(2)}) copy-start(bf16[3,75,32,256]{3,2,1,0:T(8,128)(2,1)} %vel.3) | copy-start | bytes 11059204
  15.1 7.6 %collective-permute-start.2 = (bf16[248,128]{1,0:T(8,128)(2,1)S(1)}, bf16[248,128]{1,0:T(8,128)(2,1)S(1)}, u32[]{:S(2)}, u32[]{:S(2)}) collective-permute-start(bf16[248,128]{1,0:T(8,128)(2,1)S(1)} %get-tuple-element.33), channel_id=1, source_target_pairs={{0,4},{1,5},{2,6},{3,7},{4,0},{5,1},{6,2},{7,3},{8,12},{9,13},{10,... | collective-permute-start | bytes 190472 | tf_op jit(solution)/shard_map/ppermute | solution.py:502
  15.4 7.3 %collective-permute-start.3 = (bf16[248,128]{1,0:T(8,128)(2,1)S(1)}, bf16[248,128]{1,0:T(8,128)(2,1)S(1)}, u32[]{:S(2)}, u32[]{:S(2)}) collective-permute-start(bf16[248,128]{1,0:T(8,128)(2,1)S(1)} %get-tuple-element.34), channel_id=1, source_target_pairs={{0,28},{1,29},{2,30},{3,31},{4,8},{5,9},{6,10},{7,11},{8,4},{9,5},... | collective-permute-start | bytes 190472 | tf_op jit(solution)/shard_map/ppermute | solution.py:502

commit v2 on v1

--- a/solution.py
+++ b/solution.py
@@ -53,7 +53,7 @@
 
 def pack_kernel(
     vel, off, cel, counts, moves, q1, q2, lonrec, record, rank0, total,
-    low, high, offv, celv, movev, strips, recs, sems, small,
+    low, high, offv, celv, movev, strips, recs, picked, sems, small,
 ):
     depth, rows = vel.shape[1], vel.shape[2]
     tiles = vel.shape[3] // LANES
@@ -69,11 +69,13 @@
     copies = []
     for comp in range(3):
         copies.append(
-            pltpu.make_async_copy(vel.at[comp, :, pl.ds(0, 8), :], low.at[comp], sems.at[0, comp])
+            pltpu.make_async_copy(vel.at[comp, :, pl.ds(0, 2), :], low.at[comp, :, pl.ds(0, 2), :], sems.at[0, comp])
         )
         copies.append(
             pltpu.make_async_copy(
-                vel.at[comp, :, pl.ds(rows - 8, 8), :], high.at[comp], sems.at[1, comp]
+                vel.at[comp, :, pl.ds(rows - 2, 2), :],
+                high.at[comp, :, pl.ds(6, 2), :],
+                sems.at[1, comp],
             )
         )
     for copy in copies:
@@ -114,7 +116,7 @@
         jnp.where(rank[g : g + 1] == target, 1.0, 0.0).astype(BF16) for g in range(1, 5)
     ]
     lonrec[...] = nt(packed, jnp.concatenate(placing[:2], axis=0)).astype(BF16)
-    latrec = nt(packed, jnp.concatenate(placing[2:], axis=0)).astype(BF16)
+    latrec = nt(packed, jnp.concatenate(placing[2:], axis=0))
     total[...] = carry[0:1, :].astype(I32)
     for comp in range(3):
         copies[2 * comp].wait()
@@ -131,22 +133,53 @@
             return 0
 
         lax.fori_loop(0, depth, spread, 0, unroll=15)
+    seconds = [
+        strips[pl.ds((tile * 8 + 1) * stride, planes), :].astype(BF16) for tile in range(tiles)
+    ]
+    lane = iota((1, LANES), 1)
+    south_i, south_k = latrec[9:10], latrec[11:12]
+    column = jnp.where(lane < HALF, pltpu.roll(south_i, HALF, 1), south_i + 1.0).astype(I32)
+    level = jnp.where(lane < HALF, pltpu.roll(south_k, HALF, 1), south_k).astype(I32)
+    at_column = jnp.zeros((planes, LANES), F32)
+    for tile in range(tiles):
+        where = jnp.where(iota((LANES, LANES), 0) + tile * LANES == column, 1.0, 0.0).astype(BF16)
+        at_column = at_column + jnp.dot(seconds[tile], where, preferred_element_type=F32)
+    picked[0:planes, :] = at_column
+    deep = up8(depth)
+    carried = []
+    for step in range(2):
+        for comp in range(3):
+            lines = picked[pl.ds(comp, deep, stride=3), :]
+            there = iota((deep, LANES), 0) == level + step
+            carried.append(jnp.sum(jnp.where(there, lines, 0.0), axis=0, keepdims=True))
+    for n, row in enumerate(carried):
+        recs[n : n + 1, 0:LANES] = row
+    recs[len(carried) :, 0:LANES] = jnp.zeros((REC - len(carried), LANES), F32)
+    corner = nt(jnp.where(iota((REC, LANES), 1) == 0, 1.0, 0.0).astype(BF16), seconds[0])
     odd = lax.rem(lax.axis_index("lat"), 2)
     for n, out in enumerate((q1, q2)):
         upper = odd if n == 0 else 1 - odd
         for tile in range(tiles):
             last = ((tiles + tile) * 8 + 7) * stride
-            for line in range(2):
-                first = jnp.where(upper == 1, (tile * 8 + line) * stride, last)
-                at = (line * tiles + tile) * planes
-                out[at : at + planes, :] = strips[pl.ds(first, planes), :].astype(BF16)
-        out[2 * tiles * planes :, :] = latrec
+            first = jnp.where(upper == 1, tile * 8 * stride, last)
+            out[tile * planes : (tile + 1) * planes, :] = strips[pl.ds(first, planes), :].astype(BF16)
+        at = tiles * planes
+        out[at : at + REC, :] = latrec.astype(BF16)
+        out[at + REC : at + 2 * REC, :] = recs[:, 0:LANES].astype(BF16)
+        out[at + 2 * REC : at + 3 * REC, :] = corner[:, 0:LANES].astype(BF16)
+        out[at + 3 * REC :, 0 : planes - LANES] = corner[:, LANES:planes].astype(BF16)
 
 
 def table_kernel(
-    vel, record, rank0, total, first, last, seam, table, stay, index, lines, wide
+    source, record, rank0, total, first, last, seam, table, stay, index, vel, lines, wide, sems
 ):
     depth, rows, cols = vel.shape[1:]
+    parts = 1
+    step = depth // parts
+    for comp in range(3):
+        for part in range(parts):
+            at = pl.ds(part * step, step)
+            pltpu.make_async_copy(source.at[comp, at], vel.at[comp, at], sems.at[comp]).start()
     slots = record.shape[1]
     tiles = cols // LANES
     planes = up8(3 * depth)
@@ -178,6 +211,7 @@
     index[2:3, :] = odd_one.astype(I32)
     index[3:4, :] = jnp.tile(total[...], (1, slots // LANES))
     for comp in range(3):
+        pltpu.make_async_copy(source.at[comp], vel.at[comp], sems.at[comp]).wait()
         got = nt(select, vel[comp].reshape(depth * rows, cols))
         for n in range(5):
             for q in range(chunks):
@@ -258,11 +292,16 @@
         b = q2r[n * planes : (n + 1) * planes, :].astype(F32)
         return jnp.where(even_lat == north, a, b)
 
-    north0, north1, second0 = strip(True, 0), strip(True, 1), strip(True, 2)
-    south0 = strip(False, 0)
+    north0, north1, south0 = strip(True, 0), strip(True, 1), strip(False, 0)
+    second0 = []
+    for n in range(2):
+        at = 2 * planes + (2 + n) * REC
+        line = jnp.where(even_lat, q1r[at : at + REC, :], q2r[at : at + REC, :]).astype(F32)
+        second0.append(jnp.transpose(jnp.broadcast_to(line[0:1], (LANES, LANES))))
+    second0 = jnp.concatenate([second0[0], second0[1][0 : planes - LANES]], axis=0)
     west = first[...]
     west = jnp.where(lane == 32, pltpu.roll(north0, 32, 1), west)
-    west = jnp.where(lane == 33, pltpu.roll(second0, 33, 1), west)
+    west = jnp.where(lane == 33, second0, west)
     west = jnp.where(lane == 34, pltpu.roll(south0, 34, 1), west)
     west = jnp.where(lane == 35, pltpu.roll(north1, 36, 1), west)
     west = jnp.where(lane == 96, pltpu.roll(north0, 95, 1), west).astype(BF16)
@@ -307,7 +346,7 @@
             flat(12, 35),
             jnp.where(u == cols, flat(13, 33), jnp.where(u > cols, flat(13, 34), row_at(4, u))),
         )
-        second = jnp.where(x == cols, flat(12, 33), row_at(6, x))
+        second = flat(12, 33)
         south = jnp.where(x == cols, flat(12, 34), row_at(8, x))
         where = jnp.where(
             y < 0,
@@ -336,7 +375,7 @@
     even_lat = lax.rem(lat, 2) == 0
     even_lon = lax.rem(lax.axis_index("lon"), 2) == 0
     top = lat == lat_size - 1
-    both = 4 * planes
+    both = 2 * planes
 
     def pick(flag, a, b, at, size):
         return jnp.where(flag, a[at : at + size, :], b[at : at + size, :]).astype(F32)
@@ -363,6 +402,7 @@
     srec = pick(even_lat, q2r, q1r, both, REC)
     nrec = pick(even_lat, q1r, q2r, both, REC)
     nrec = jnp.where(top, nrec, pltpu.roll(nrec, HALF, 1))
+    carried = pick(even_lat, q1r, q2r, both + REC, REC)[0:8]
     groups = []
     for g, raw in enumerate((wrec, erec, srec, nrec)):
         raw = jnp.where(inside, raw, 0.0)
@@ -387,7 +427,6 @@
         put(t, pick(even_lat, q2, q1, at, planes))
         put(2 + t, pick(even_lat, q1, q2, at, planes))
         put(4 + t, pick(even_lat, q1r, q2r, at, planes))
-        put(6 + t, pick(even_lat, q1r, q2r, at + 2 * planes, planes))
         put(8 + t, pick(even_lat, q2r, q1r, at, planes))
     put(10, first[...])
     put(11, last[...])
@@ -429,6 +468,10 @@
                 e = idxs[4 * g + q, t]
                 value = pltpu.roll(table[pl.ds(e >> SHIFT, 8), :], (t - e) & (LANES - 1), 1)
                 total = jnp.where(lane == t, value, total)
+            if g == 3 and q > 1:
+                sent = carried if q == 2 else pltpu.roll(carried, HALF, 1)
+                beyond = top if q == 2 else top | (raw[9:10].astype(I32) == cols - 1)
+                total = jnp.where(beyond, total, sent)
             acc.append(pltpu.roll(total * signs[q], base & (LANES - 1), 1))
         moved = pltpu.roll(raw, base & (LANES - 1), 1)
         values = decode(moved) + [moved[9:10], moved[10:11], moved[11:12]]
@@ -496,7 +539,7 @@
     planes = up8(3 * depth)
     stride = odd_stride(depth)
     tiles = cols // LANES
-    high = 2 * tiles * planes + REC
+    high = tiles * planes + 4 * REC
 
     def send(x, partner):
         return lax.ppermute(x, axes, route(lon_size, lat_size, partner))
@@ -524,6 +567,7 @@
             pltpu.VMEM((1, slots), I32),
             pltpu.VMEM((2 * tiles * 8 * stride, LANES), F32),
             pltpu.VMEM((REC, slots), F32),
+            pltpu.VMEM((3 * up8(depth) + 8, LANES), F32),
             pltpu.SemaphoreType.DMA((2, 3)),
             pltpu.SemaphoreType.DMA((3,)),
         ],
@@ -552,16 +596,18 @@
             array((8, slots), F32),
             array((4, slots), I32),
         ),
-        in_specs=[VMEM] * 4,
+        in_specs=[HBM] + [VMEM] * 3,
         out_specs=(VMEM,) * 6,
         scratch_shapes=[
+            pltpu.VMEM((3, depth, rows, cols), BF16),
             pltpu.VMEM((5 * deep, LANES), F32),
             pltpu.VMEM((9 * up8(per * deep), LANES), F32),
+            pltpu.SemaphoreType.DMA((3,)),
         ],
         compiler_params=room(20),
         cost_estimate=pl.CostEstimate(flops=10**9, bytes_accessed=2 * velocity.size, transcendentals=0),
         name="table",
-    )(pltpu.with_memory_space_constraint(velocity, pltpu.VMEM), record, rank0, total)
+    )(pltpu.with_memory_space_constraint(velocity, pltpu.HBM), record, rank0, total)
     p1, p2 = pl.pallas_call(
         side_kernel,
         out_shape=(array((planes + REC, LANES), BF16), array((planes + REC, LANES), BF16)),

time: 26.2 us -> 24 us (0.916); the launches traced: 26.6 us -> 23.6 us
  local copies, waits for them, and re-layouts: 2.04 us -> 0 us
  Pallas kernels: 12.9 us -> 11.4 us
  waiting for transfers between devices: 0.01 us -> 0.77 us
    pallas_call x1, Pallas kernels: 4.16 us -> 2.09 us  [shards(): pl.pallas_call(functools.partial(gather_kernel, stride), out_shape=(array...]
    unnamed x2 -> x0, local copies, waits for them, and re-layouts: 2.04 us -> none
    pallas_call x1, Pallas kernels: 2.58 us -> 3.58 us  [shards(): pl.pallas_call(table_kernel, out_shape=(array((planes, LANES), F32), arra...]
    ppermute x4, waiting for transfers between devices: 0.01 us -> 0.77 us  [send(): return lax.ppermute(x, axes, route(lon_size, lat_size, partner))]
    pallas_call x1, Pallas kernels: 2.06 us -> 1.8 us  [shards(): pl.pallas_call(pack_kernel, out_shape=(array((high, LANES), BF16), array(...]
  transfers between devices with their start and end apart: 4 -> 4, of which waited for: 0 -> 1; matrix products, arithmetic and copies ran while one was open for 0% -> 0% of each run, Pallas kernels for 25% -> 24%
where the time goes in v2:
time: 24 us; the launch traced here: 23.6 us
  Pallas kernels  11.4 us (48%)
  starting transfers between devices  10.1 us (42%)
  between operations  1.34 us (6%)
  waiting for transfers between devices  0.77 us (3%)
    ppermute x4, starting transfers between devices, send(): return lax.ppermute(x, axes, route(lon_size, lat_size, partner))  10.1 us
    pallas_call x1, Pallas kernels, shards(): pl.pallas_call(functools.partial(final_kernel, rows, cols, lat_size), out...  3.67 us
    pallas_call x1, Pallas kernels, shards(): pl.pallas_call(table_kernel, out_shape=(array((planes, LANES), F32), arra...  3.58 us
    pallas_call x1, Pallas kernels, shards(): pl.pallas_call(functools.partial(gather_kernel, stride), out_shape=(array...  2.09 us
    pallas_call x1, Pallas kernels, shards(): pl.pallas_call(pack_kernel, out_shape=(array((high, LANES), BF16), array(...  1.8 us
    ppermute x4, waiting for transfers between devices, send(): return lax.ppermute(x, axes, route(lon_size, lat_size, partner))  0.77 us
  transfers between devices with their start and end apart: 4, of which 1 were waited for; matrix products, arithmetic and copies ran while one was open for 0% of the time, Pallas kernels for 24%

profile of v2, /device:TPU:3, one launch (start us, length us, event | category | flops | bytes accessed | tf_op | source)
XLA Modules:
  0.0 23.6 jit_solution(3837035827039158242)
XLA Ops:
  1.3 1.8 %pack.1 = (bf16[528,128]{1,0:T(8,128)(2,1)S(1)}, bf16[528,128]{1,0:T(8,128)(2,1)S(1)}, bf16[16,128]{1,0:T(8,128)(2,1)S(1)}, bf16[16,768]{1,0:T(8,128)(2,1)S(1)},...) custom-call(bf16[3,75,32,256]{3,2,1,0:T(8,128)(2,1)} %source.1, f32[3,1,768]{2,1,0:T(1,128)} %off.1, s32[3,1,768]{2,1,0:T(1,128)} %cel.1, ...), custom_call_target="tpu_custom_call" | custom-call | tf_op jit(solution)/shard_map/pack/pallas_call | solution.py:550
  3.1 0.7 %collective-permute-start = (bf16[528,128]{1,0:T(8,128)(2,1)S(1)}, bf16[528,128]{1,0:T(8,128)(2,1)S(1)}, u32[]{:S(2)}, u32[]{:S(2)}) collective-permute-start(bf16[528,128]{1,0:T(8,128)(2,1)S(1)} %get-tuple-element.30.q1), channel_id=1, source_target_pairs={{0,1},{1,0},{2,3},{3,2},{4,5},{5,4},{6,7},{7,6},{8,9},{9,8},{10,11... | collective-permute-start | bytes 405512 | tf_op jit(solution)/shard_map/ppermute | solution.py:545
  3.8 6.2 %collective-permute-start.1 = (bf16[528,128]{1,0:T(8,128)(2,1)S(1)}, bf16[528,128]{1,0:T(8,128)(2,1)S(1)}, u32[]{:S(2)}, u32[]{:S(2)}) collective-permute-start(bf16[528,128]{1,0:T(8,128)(2,1)S(1)} %get-tuple-element.31.q2), channel_id=1, source_target_pairs={{1,2},{2,1},{3,31},{5,6},{6,5},{7,27},{9,10},{10,9},{11,23},{13,14... | collective-permute-start | bytes 405512 | tf_op jit(solution)/shard_map/ppermute | solution.py:545
  10.0 3.6 %table.1 = (f32[232,128]{1,0:T(8,128)S(1)}, f32[232,128]{1,0:T(8,128)S(1)}, f32[232,128]{1,0:T(8,128)S(1)}, f32[15153,128]{1,0:T(8,128)S(1)}, f32[8,768]{1,0:T(8,128)S(1)}, /*index=5*/s32[4,768]{1,0:T(4,128)S(1)}) custom-call(bf16[3,75,32,256]{3,2,1,0:T(8,128)(2,1)} %source.1, bf16[16,768]{1,0:T(8,128)(2,1)S(1)} %get-tuple-element.19.record, ...), custom_call_target="tpu_custom_call" | custom-call | flops 1000000000 | bytes 3686400 | tf_op jit(solution)/shard_map/table/pallas_call | solution.py:589
  13.6 0.0 collective-permute-done.q1r
  13.6 0.0 collective-permute-done.1.q2r
  13.6 0.3 %sides.1 = (bf16[248,128]{1,0:T(8,128)(2,1)S(1)}, bf16[248,128]{1,0:T(8,128)(2,1)S(1)}) custom-call(f32[232,128]{1,0:T(8,128)S(1)} %get-tuple-element.27.first, f32[232,128]{1,0:T(8,128)S(1)} %get-tuple-element.28.last, bf16[16,128]{1,0:T(8,128)(2,1)S(1)} %get-tuple-element.32.lonrec, bf16[528,128]{1,0:T(8,128)(2,1)S(1)} %collective-permute-done.q1r, ...), custom_call_target="tpu_custom_call" | custom-call | tf_op jit(solution)/shard_map/sides/pallas_call | solution.py:611
  13.9 0.3 %collective-permute-start.2 = (bf16[248,128]{1,0:T(8,128)(2,1)S(1)}, bf16[248,128]{1,0:T(8,128)(2,1)S(1)}, u32[]{:S(2)}, u32[]{:S(2)}) collective-permute-start(bf16[248,128]{1,0:T(8,128)(2,1)S(1)} %get-tuple-element.33), channel_id=1, source_target_pairs={{0,4},{1,5},{2,6},{3,7},{4,0},{5,1},{6,2},{7,3},{8,12},{9,13},{10,... | collective-permute-start | bytes 190472 | tf_op jit(solution)/shard_map/ppermute | solution.py:545
  14.2 2.9 %collective-permute-start.3 = (bf16[248,128]{1,0:T(8,128)(2,1)S(1)}, bf16[248,128]{1,0:T(8,128)(2,1)S(1)}, u32[]{:S(2)}, u32[]{:S(2)}) collective-permute-start(bf16[248,128]{1,0:T(8,128)(2,1)S(1)} %get-tuple-element.34), channel_id=1, source_target_pairs={{0,28},{1,29},{2,30},{3,31},{4,8},{5,9},{6,10},{7,11},{8,4},{9,5},... | collective-permute-start | bytes 190472 | tf_op jit(solution)/shard_map/ppermute | solution.py:545
  17.1 2.1 %gather.1 = (f32[4,6,8,128]{3,2,1,0:T(8,128)S(1)}, s32[896]{0:T(1024)S(1)}) custom-call(f32[15153,128]{1,0:T(8,128)S(1)} %get-tuple-element.23.table, s32[4,768]{1,0:T(4,128)S(1)} %get-tuple-element.24.index), custom_call_target="tpu_custom_call" | custom-call | flops 1000000000 | bytes 3686400 | tf_op jit(solution)/shard_map/gather/pallas_call | solution.py:621
  19.2 0.0 collective-permute-done.2.p1r
  19.2 0.8 %collective-permute-done.3.p2r = bf16[248,128]{1,0:T(8,128)(2,1)S(1)} collective-permute-done((bf16[248,128]{1,0:T(8,128)(2,1)S(1)}, bf16[248,128]{1,0:T(8,128)(2,1)S(1)}, u32[]{:S(2)}, u32[]{:S(2)}) %collective-permute-start.3) | collective-permute-done | bytes 63520 | tf_op jit(solution)/shard_map/ppermute | solution.py:545
  20.0 3.7 %final.1 = (f32[3,1,768]{2,1,0:T(1,128)}, s32[3,1,768]{2,1,0:T(1,128)}, s32[1,1]{1,0:T(1,128)}) custom-call(f32[8,768]{1,0:T(8,128)S(1)} %get-tuple-element.22.stay, f32[4,6,8,128]{3,2,1,0:T(8,128)S(1)} %get-tuple-element.25.got, s32[896]{0:T(1024)S(1)} %get-tuple-element.26.listed_any, f32[232,128]{1,0:T(8,128)S(1)} %get-tuple-element.27.first, ...), custom_call_target="tpu_custom_call" | custom-call | tf_op jit(solution)/shard_map/final/pallas_call | solution.py:633
Async XLA Ops:
  3.1 10.5 %collective-permute-start = (bf16[528,128]{1,0:T(8,128)(2,1)S(1)}, bf16[528,128]{1,0:T(8,128)(2,1)S(1)}, u32[]{:S(2)}, u32[]{:S(2)}) collective-permute-start(bf16[528,128]{1,0:T(8,128)(2,1)S(1)} %get-tuple-element.30.q1), channel_id=1, source_target_pairs={{0,1},{1,0},{2,3},{3,2},{4,5},{5,4},{6,7},{7,6},{8,9},{9,8},{10,11... | collective-permute-start | bytes 405512 | tf_op jit(solution)/shard_map/ppermute | solution.py:545
  3.8 9.8 %collective-permute-start.1 = (bf16[528,128]{1,0:T(8,128)(2,1)S(1)}, bf16[528,128]{1,0:T(8,128)(2,1)S(1)}, u32[]{:S(2)}, u32[]{:S(2)}) collective-permute-start(bf16[528,128]{1,0:T(8,128)(2,1)S(1)} %get-tuple-element.31.q2), channel_id=1, source_target_pairs={{1,2},{2,1},{3,31},{5,6},{6,5},{7,27},{9,10},{10,9},{11,23},{13,14... | collective-permute-start | bytes 405512 | tf_op jit(solution)/shard_map/ppermute | solution.py:545
  13.9 5.3 %collective-permute-start.2 = (bf16[248,128]{1,0:T(8,128)(2,1)S(1)}, bf16[248,128]{1,0:T(8,128)(2,1)S(1)}, u32[]{:S(2)}, u32[]{:S(2)}) collective-permute-start(bf16[248,128]{1,0:T(8,128)(2,1)S(1)} %get-tuple-element.33), channel_id=1, source_target_pairs={{0,4},{1,5},{2,6},{3,7},{4,0},{5,1},{6,2},{7,3},{8,12},{9,13},{10,... | collective-permute-start | bytes 190472 | tf_op jit(solution)/shard_map/ppermute | solution.py:545
  14.2 5.8 %collective-permute-start.3 = (bf16[248,128]{1,0:T(8,128)(2,1)S(1)}, bf16[248,128]{1,0:T(8,128)(2,1)S(1)}, u32[]{:S(2)}, u32[]{:S(2)}) collective-permute-start(bf16[248,128]{1,0:T(8,128)(2,1)S(1)} %get-tuple-element.34), channel_id=1, source_target_pairs={{0,28},{1,29},{2,30},{3,31},{4,8},{5,9},{6,10},{7,11},{8,4},{9,5},... | collective-permute-start | bytes 190472 | tf_op jit(solution)/shard_map/ppermute | solution.py:545
